TPU v7x, 32 devices: a whole 2x2x4 slice. The times are simulated.
32 devices in a mesh: space: 8 (over z, y), scene: 4 (over x, core).
Axes of the slice: x: 2, y: 2, z: 4, core: 2. Of those that a mesh axis runs over, the one named last changes fastest.
Arguments:
- features: bfloat16 [4, 16, 64, 512], P('scene', 'space'), may hold values from -6 to 6
- cotangent: bfloat16 [4, 16, 64, 512], P('scene', 'space'), may hold values from -6 to 6
- weight: bfloat16 [27, 64, 64], replicated, may hold values from -0.15625 to 0.15625
- neighbours: int32 [4, 16, 27], P('scene', 'space'), may hold values from -1 to 15, as said below
- occupancy: int32 [4, 16, 512], P('scene', 'space'), may hold values 0 or 1
Outputs:
- conv_out: bfloat16 [4, 16, 64, 512], P('scene', 'space')
- grad_features: bfloat16 [4, 16, 64, 512], P('scene', 'space')
- grad_weight: float32 [27, 64, 64], replicated
Inputs may be any that keep to these rules, and one draw needn't show every extreme that they name: neighbours[s, b, 9 (a + 1) + 3 (c + 1) + (e + 1)] is the number within scene s of the active brick whose brick coordinates differ from brick b's by (a, c, e), each in -1, 0, 1, or -1 where no such brick is active; entry 13 is b itself and the relation is symmetric. Bricks 2 p to 2 (p + 1) - 1 form block p, a slab along the first brick coordinate: a neighbour at offset a = 0 lies in block p, a neighbour in block p - 1 has offset a = -1, a neighbour in block p + 1 has offset a = +1, and no neighbour lies in any other block.
All inputs are finite; a program needn't handle non-finite values. No bound on the sum of `occupancy` on one device may be relied on, other than what follows from the above.
Results may differ from a plain program's by a relative error of at most 0.001.
Values may be sent and summed in bfloat16 or wider, within the bound.
No kernel may reach another device: no remote copies, remote signals or barrier semaphores. Data moves between devices by JAX's collectives and lax.ppermute only.
A program may use at most 64 MiB of HBM per device.

v0:
```python
import math
import jax
import jax.numpy as jnp
from jax import lax
from jax.sharding import PartitionSpec as P


def with_halo(cells, sides, width):
    for axis, dim in sides:
        count = lax.axis_size(axis)
        ends = count - 1
        head = lax.slice_in_dim(cells, 0, width, axis=dim)
        tail = lax.slice_in_dim(cells, cells.shape[dim] - width, cells.shape[dim], axis=dim)
        cells = jnp.concatenate(
            [
                lax.ppermute(tail, axis, [(i, (i + 1) % count) for i in range(ends)]),
                cells,
                lax.ppermute(head, axis, [((i + 1) % count, i) for i in range(ends)]),
            ],
            axis=dim,
        )
    return cells


def bounds(offset):
    if offset == 0:
        return (7, 8)
    if offset == 1:
        return (0, 8)
    return (0, 1)


def assemble(lookup, places):
    plane_list = []
    for off_x in range(3):
        x_low, x_high = bounds(off_x)
        row_list = []
        for off_y in range(3):
            y_low, y_high = bounds(off_y)
            cell_list = []
            for off_z in range(3):
                z_low, z_high = bounds(off_z)
                section = lookup[:, :, x_low:x_high, y_low:y_high, z_low:z_high]
                cell_list.append(
                    jnp.take(section, places[:, 9 * off_x + 3 * off_y + off_z], axis=0)
                )
            row_list.append(jnp.concatenate(cell_list, axis=4))
        plane_list.append(jnp.concatenate(row_list, axis=3))
    return jnp.concatenate(plane_list, axis=2)


def window(volume, start_x, start_y, start_z):
    bricks, channels = (volume.shape[0], volume.shape[1])
    return volume[
        :, :, start_x : start_x + 8, start_y : start_y + 8, start_z : start_z + 8
    ].reshape(bricks, channels, 512)


def local(features, cotangent, weight, neighbours, occupancy):
    bricks, channels = (features.shape[1], features.shape[2])
    grad_scale = 1.0 / math.sqrt(lax.axis_size("scene") * bricks * lax.axis_size("space") * 512)
    present = occupancy[0].astype(jnp.bfloat16)[:, None, :]
    masked_x = features[0] * present
    masked_gradient = cotangent[0] * present
    stacked = jnp.stack([masked_x, masked_gradient])
    gathered = with_halo(stacked, (("space", 1),), bricks)
    zero_rows = jnp.zeros((2, 1, channels, 512), jnp.bfloat16)
    lookup = jnp.concatenate([gathered, zero_rows], axis=1).reshape(
        2, 3 * bricks + 1, channels, 8, 8, 8
    )
    offset_base = (lax.axis_index("space") - 1) * bricks
    places = jnp.where(neighbours[0] < 0, 3 * bricks, neighbours[0] - offset_base)
    volume_x = assemble(lookup[0], places)
    volume_g = assemble(lookup[1], places)
    acc_y = jnp.zeros((bricks, channels, 512), jnp.float32)
    acc_g = jnp.zeros((bricks, channels, 512), jnp.float32)
    partial_w = []
    for tap_x in range(3):
        fwd_list = []
        back_list = []
        back_weights = []
        for inner_tap in range(9):
            tap_y, tap_z = (inner_tap // 3, inner_tap % 3)
            fwd_list.append(window(volume_x, tap_x, tap_y, tap_z))
            back_list.append(window(volume_g, 2 - tap_x, 2 - tap_y, 2 - tap_z))
            back_weights.append(weight[9 * tap_x + inner_tap].T)
        forward_stacked_taps = jnp.concatenate(fwd_list, axis=1)
        backward_stacked_taps = jnp.concatenate(back_list, axis=1)
        forward_kernel_weight = weight[9 * tap_x : 9 * tap_x + 9].reshape(9 * channels, channels)
        backward_kernel_weight = jnp.concatenate(back_weights, axis=0)
        acc_y = acc_y + jnp.einsum(
            "hpo,ps->hso",
            forward_stacked_taps,
            forward_kernel_weight,
            preferred_element_type=jnp.float32,
        )
        acc_g = acc_g + jnp.einsum(
            "ish,sw->iwh",
            backward_stacked_taps,
            backward_kernel_weight,
            preferred_element_type=jnp.float32,
        )
        grouped_weight = jnp.einsum(
            "hgm,htm->gt", forward_stacked_taps, masked_gradient, preferred_element_type=jnp.float32
        )
        partial_w.append(grouped_weight.reshape(9, channels, channels))
    mask_wide = present.astype(jnp.float32)
    out_y = (acc_y * mask_wide).astype(jnp.bfloat16)[None]
    out_g = (acc_g * mask_wide).astype(jnp.bfloat16)[None]
    grad_w = jnp.concatenate(partial_w, axis=0) * grad_scale
    by_scene = lax.psum(grad_w, "scene")
    summed = lax.psum(by_scene, "space")
    return (out_y, out_g, summed)


def solution(mesh):
    in_specs = (
        P("scene", "space", None, None),
        P("scene", "space", None, None),
        P(),
        P("scene", "space", None),
        P("scene", "space", None),
    )
    out_specs = (P("scene", "space", None, None), P("scene", "space", None, None), P())
    return jax.shard_map(local, mesh=mesh, in_specs=in_specs, out_specs=out_specs, check_vma=False)
```

profile of v0, /device:TPU:0, one launch (start us, length us, event | category | flops | bytes accessed | tf_op | source)
XLA Modules:
  0.0 337.7 jit_solution(2646253069375196064)
XLA Ops:
  8.3 1.3 fusion.14
  11.0 1.3 collective-permute-start.1
  12.3 5.6 %collective-permute-start = (bf16[2,2,64,512]{2,3,1,0:T(8,128)(2,1)S(1)}, bf16[2,2,64,512]{2,3,1,0:T(8,128)(2,1)S(1)}, u32[]{:S(2)}, u32[]{:S(2)}) collective-permute-start(bf16[2,2,64,512]{2,3,1,0:T(8,128)(2,1)S(1)} %pad_maximum_fusion), channel_id=1, source_target_pairs={{0,4},{4,8},{8,12},{12,16},{16,20},{20,24},{24,28},{1,5},{5,9},{9,... | collective-permute-start | bytes 786440 | tf_op jit(solution)/shard_map/ppermute | solution.py:16
  53.5 1.3 gather_fusion.35
  54.7 1.3 gather_fusion.17
  58.3 1.3 gather_fusion.33
  59.6 1.3 gather_fusion.15
  85.2 1.5 fusion.23
  88.5 1.7 copy.240
  90.2 1.7 copy.241
  91.9 1.7 copy.242
  93.7 1.7 copy.243
  95.4 1.7 copy.244
  97.1 1.7 copy.245
  98.8 1.7 copy.246
  100.6 1.7 copy.247
  103.3 1.8 copy.251
  105.0 1.6 constant_dynamic-update-slice_fusion.17
  106.6 1.7 copy.252
  108.3 1.7 copy.253
  113.3 1.8 copy.257
  135.8 1.2 fusion.22
  137.1 1.7 copy.272
  138.8 1.6 constant_dynamic-update-slice_fusion.26
  140.4 1.7 copy.273
  142.1 1.7 copy.274
  151.4 1.5 fusion.21
  152.9 1.7 copy.303
  154.6 1.6 constant_dynamic-update-slice_fusion.35
  156.2 1.7 copy.304
  157.9 1.7 copy.305
  159.6 1.7 copy.306
  161.4 1.7 copy.307
  163.1 1.7 copy.308
  164.8 1.7 copy.309
  166.6 1.7 copy.310
  170.0 1.8 copy.314
  171.8 1.6 constant_dynamic-update-slice_fusion.44
  173.4 1.7 copy.315
  187.8 1.3 fusion.20
  189.1 1.7 copy.329
  190.8 1.6 constant_dynamic-update-slice_fusion.53
  192.4 1.7 copy.330
  205.0 1.8 convolution_bitcast_fusion
  219.7 29.3 %all-reduce.3.cloned.1.call-done = f32[27,64,64]{2,1,0:T(8,128)} async-done(((f32[27,64,64]{2,1,0:T(8,128)}), f32[27,64,64]{2,1,0:T(8,128)}) %all-reduce.3.cloned.1.call-update) | async-done | bytes 442384 | tf_op jit(solution)/shard_map/psum | solution.py:111
  249.9 2.3 fusion.5
  252.2 76.5 %all-reduce.5.cloned.1.call-done = f32[27,64,64]{2,1,0:T(8,128)} async-done(((f32[27,64,64]{2,1,0:T(8,128)}), f32[27,64,64]{2,1,0:T(8,128)}) %all-reduce.5.cloned.1.call-update) | async-done | bytes 442384 | tf_op jit(solution)/shard_map/psum | solution.py:112
  328.7 2.2 copy.476
  (636 shorter events, 136.0 us)
Async XLA Ops:
  7.2 241.8 %all-reduce.3.cloned.1.call-start = ((), (), s32[]{:S(2)}) async-start(), calls=%async_computation | async-start | bytes 1769472 | tf_op jit(solution)/shard_map/psum | solution.py:111
  10.7 16.3 %copy-start.1 = (bf16[27,64,64]{2,1,0:T(8,128)(2,1)S(1)}, bf16[27,64,64]{2,1,0:T(8,128)(2,1)}, u32[]{:S(2)}) copy-start(bf16[27,64,64]{2,1,0:T(8,128)(2,1)} %param.23) | copy-start | bytes 663556
  11.0 32.9 %collective-permute-start.1 = (bf16[2,2,64,512]{2,3,1,0:T(8,128)(2,1)S(1)}, bf16[2,2,64,512]{2,3,1,0:T(8,128)(2,1)S(1)}, u32[]{:S(2)}, u32[]{:S(2)}) collective-permute-start(bf16[2,2,64,512]{2,3,1,0:T(8,128)(2,1)S(1)} %pad_maximum_fusion), channel_id=1, source_target_pairs={{4,0},{8,4},{12,8},{16,12},{20,16},{24,20},{28,24},{5,1},{9,5},{13... | collective-permute-start | bytes 786440 | tf_op jit(solution)/shard_map/ppermute | solution.py:18
  12.3 31.6 %collective-permute-start = (bf16[2,2,64,512]{2,3,1,0:T(8,128)(2,1)S(1)}, bf16[2,2,64,512]{2,3,1,0:T(8,128)(2,1)S(1)}, u32[]{:S(2)}, u32[]{:S(2)}) collective-permute-start(bf16[2,2,64,512]{2,3,1,0:T(8,128)(2,1)S(1)} %pad_maximum_fusion), channel_id=1, source_target_pairs={{0,4},{4,8},{8,12},{12,16},{16,20},{20,24},{24,28},{1,5},{5,9},{9,... | collective-permute-start | bytes 786440 | tf_op jit(solution)/shard_map/ppermute | solution.py:16
  67.3 9.0 %copy-start.128 = (pred[2]{0:T(512)(128)(4,1)S(1)}, pred[2]{0:T(512)(128)(4,1)}, u32[]{:S(2)}) copy-start(pred[2]{0:T(512)(128)(4,1)} %get-tuple-element.270) | copy-start | bytes 10
  68.7 8.4 %copy-start.122 = (pred[2]{0:T(512)(128)(4,1)S(1)}, pred[2]{0:T(512)(128)(4,1)}, u32[]{:S(2)}) copy-start(pred[2]{0:T(512)(128)(4,1)} %get-tuple-element.271) | copy-start | bytes 10
  68.7 8.5 %copy-start.108 = (bf16[7,64]{1,0:T(8,128)(2,1)S(1)}, bf16[7,64]{1,0:T(8,128)(2,1)}, u32[]{:S(2)}) copy-start(bf16[7,64]{1,0:T(8,128)(2,1)} %get-tuple-element.48) | copy-start | bytes 2692
  68.7 9.2 %copy-start.134 = (pred[2]{0:T(512)(128)(4,1)S(1)}, pred[2]{0:T(512)(128)(4,1)}, u32[]{:S(2)}) copy-start(pred[2]{0:T(512)(128)(4,1)} %get-tuple-element.273) | copy-start | bytes 10
  68.7 9.9 %copy-start.124 = (pred[2]{0:T(512)(128)(4,1)S(1)}, pred[2]{0:T(512)(128)(4,1)}, u32[]{:S(2)}) copy-start(pred[2]{0:T(512)(128)(4,1)} %get-tuple-element.274) | copy-start | bytes 10
  68.7 10.0 %copy-start.107 = (bf16[7,64]{1,0:T(8,128)(2,1)S(1)}, bf16[7,64]{1,0:T(8,128)(2,1)}, u32[]{:S(2)}) copy-start(bf16[7,64]{1,0:T(8,128)(2,1)} %get-tuple-element.49) | copy-start | bytes 2692
  68.7 10.7 %copy-start.132 = (pred[2]{0:T(512)(128)(4,1)S(1)}, pred[2]{0:T(512)(128)(4,1)}, u32[]{:S(2)}) copy-start(pred[2]{0:T(512)(128)(4,1)} %get-tuple-element.275) | copy-start | bytes 10
  68.7 10.7 %copy-start.61 = (bf16[2,64,8]{1,2,0:T(8,128)(2,1)S(1)}, bf16[2,64,8]{1,2,0:T(8,128)(2,1)}, u32[]{:S(2)}) copy-start(bf16[2,64,8]{1,2,0:T(8,128)(2,1)} %gather_fusion.35) | copy-start | bytes 6148
  68.7 10.7 %copy-start.62 = (bf16[2,64,8]{1,2,0:T(8,128)(2,1)S(1)}, bf16[2,64,8]{1,2,0:T(8,128)(2,1)}, u32[]{:S(2)}) copy-start(bf16[2,64,8]{1,2,0:T(8,128)(2,1)} %gather_fusion.17) | copy-start | bytes 6148
  68.7 10.7 %copy-start.157 = (pred[2]{0:T(512)(128)(4,1)S(1)}, pred[2]{0:T(512)(128)(4,1)}, u32[]{:S(2)}) copy-start(pred[2]{0:T(512)(128)(4,1)} %get-tuple-element.245) | copy-start | bytes 10
  69.4 10.7 %copy-start.146 = (pred[2]{0:T(512)(128)(4,1)S(1)}, pred[2]{0:T(512)(128)(4,1)}, u32[]{:S(2)}) copy-start(pred[2]{0:T(512)(128)(4,1)} %get-tuple-element.246) | copy-start | bytes 10
  69.5 10.8 %copy-start.63 = (bf16[2,64,8]{1,2,0:T(8,128)(2,1)S(1)}, bf16[2,64,8]{1,2,0:T(8,128)(2,1)}, u32[]{:S(2)}) copy-start(bf16[2,64,8]{1,2,0:T(8,128)(2,1)} %gather_fusion.33) | copy-start | bytes 6148
  69.5 10.8 %copy-start.64 = (bf16[2,64,8]{1,2,0:T(8,128)(2,1)S(1)}, bf16[2,64,8]{1,2,0:T(8,128)(2,1)}, u32[]{:S(2)}) copy-start(bf16[2,64,8]{1,2,0:T(8,128)(2,1)} %gather_fusion.15) | copy-start | bytes 6148
  69.5 10.8 %copy-start.158 = (pred[2]{0:T(512)(128)(4,1)S(1)}, pred[2]{0:T(512)(128)(4,1)}, u32[]{:S(2)}) copy-start(pred[2]{0:T(512)(128)(4,1)} %get-tuple-element.247) | copy-start | bytes 10
  69.5 11.5 %copy-start.144 = (pred[2]{0:T(512)(128)(4,1)S(1)}, pred[2]{0:T(512)(128)(4,1)}, u32[]{:S(2)}) copy-start(pred[2]{0:T(512)(128)(4,1)} %get-tuple-element.248) | copy-start | bytes 10
  69.5 11.6 %copy-start.143 = (pred[2]{0:T(512)(128)(4,1)S(1)}, pred[2]{0:T(512)(128)(4,1)}, u32[]{:S(2)}) copy-start(pred[2]{0:T(512)(128)(4,1)} %get-tuple-element.249) | copy-start | bytes 10
  103.3 8.4 %copy-start.8 = (bf16[2,64,8,8,8]{1,4,3,2,0:T(8,128)(2,1)S(1)}, bf16[2,64,8,8,8]{1,4,3,2,0:T(8,128)(2,1)}, u32[]{:S(2)}) copy-start(bf16[2,64,8,8,8]{1,4,3,2,0:T(8,128)(2,1)} %get-tuple-element.178) | copy-start | bytes 393220
  112.4 8.7 %copy-start.85 = (bf16[7,64,1,8,1]{1,4,3,2,0:T(2,128)(2,1)S(1)}, bf16[7,64,1,8,1]{1,4,3,2,0:T(2,128)(2,1)}, u32[]{:S(2)}) copy-start(bf16[7,64,1,8,1]{1,4,3,2,0:T(2,128)(2,1)} %get-tuple-element.81) | copy-start | bytes 21508
  113.2 9.2 %copy-start.57 = (bf16[7,64,8,8]{1,0,3,2:T(8,128)(2,1)S(1)}, bf16[7,64,8,8]{1,0,3,2:T(8,128)(2,1)}, u32[]{:S(2)}) copy-start(bf16[7,64,8,8]{1,0,3,2:T(8,128)(2,1)} %get-tuple-element.58) | copy-start | bytes 172036
  113.3 9.2 %copy-start.5 = (bf16[7,64,8,8]{1,3,2,0:T(8,128)(2,1)S(1)}, bf16[7,64,8,8]{1,3,2,0:T(8,128)(2,1)}, u32[]{:S(2)}) copy-start(bf16[7,64,8,8]{1,3,2,0:T(8,128)(2,1)} %get-tuple-element.85) | copy-start | bytes 172036
  115.8 9.4 %copy-start.118 = (bf16[7,64,1,1,1]{1,4,3,2,0:T(2,128)(2,1)S(1)}, bf16[7,64,1,1,1]{1,4,3,2,0:T(2,128)(2,1)}, u32[]{:S(2)}) copy-start(bf16[7,64,1,1,1]{1,4,3,2,0:T(2,128)(2,1)} %get-tuple-element.72) | copy-start | bytes 2692
  115.8 9.4 %copy-start.119 = (bf16[7,64,1,1,1]{1,4,3,2,0:T(2,128)(2,1)S(1)}, bf16[7,64,1,1,1]{1,4,3,2,0:T(2,128)(2,1)}, u32[]{:S(2)}) copy-start(bf16[7,64,1,1,1]{1,4,3,2,0:T(2,128)(2,1)} %get-tuple-element.73) | copy-start | bytes 2692
  115.8 10.2 %copy-start.104 = (bf16[7,64]{1,0:T(8,128)(2,1)S(1)}, bf16[7,64]{1,0:T(8,128)(2,1)}, u32[]{:S(2)}) copy-start(bf16[7,64]{1,0:T(8,128)(2,1)} %get-tuple-element.44) | copy-start | bytes 2692
  115.8 10.8 %copy-start.89 = (bf16[7,64,8]{1,0,2:T(8,128)(2,1)S(1)}, bf16[7,64,8]{1,0,2:T(8,128)(2,1)}, u32[]{:S(2)}) copy-start(bf16[7,64,8]{1,0,2:T(8,128)(2,1)} %get-tuple-element.50) | copy-start | bytes 21508
  115.8 10.8 %copy-start.70 = (bf16[7,64,8]{1,2,0:T(8,128)(2,1)S(1)}, bf16[7,64,8]{1,2,0:T(8,128)(2,1)}, u32[]{:S(2)}) copy-start(bf16[7,64,8]{1,2,0:T(8,128)(2,1)} %get-tuple-element.78) | copy-start | bytes 21508
  115.8 12.9 %copy-start.103 = (bf16[7,64]{1,0:T(8,128)(2,1)S(1)}, bf16[7,64]{1,0:T(8,128)(2,1)}, u32[]{:S(2)}) copy-start(bf16[7,64]{1,0:T(8,128)(2,1)} %get-tuple-element.42) | copy-start | bytes 2692
  115.9 13.6 %copy-start.155 = (pred[2]{0:T(512)(128)(4,1)S(1)}, pred[2]{0:T(512)(128)(4,1)}, u32[]{:S(2)}) copy-start(pred[2]{0:T(512)(128)(4,1)} %get-tuple-element.236) | copy-start | bytes 10
  115.9 14.2 %copy-start.153 = (pred[2]{0:T(512)(128)(4,1)S(1)}, pred[2]{0:T(512)(128)(4,1)}, u32[]{:S(2)}) copy-start(pred[2]{0:T(512)(128)(4,1)} %get-tuple-element.237) | copy-start | bytes 10
  116.7 14.1 %copy-start.154 = (pred[2]{0:T(512)(128)(4,1)S(1)}, pred[2]{0:T(512)(128)(4,1)}, u32[]{:S(2)}) copy-start(pred[2]{0:T(512)(128)(4,1)} %get-tuple-element.238) | copy-start | bytes 10
  116.7 14.7 %copy-start.152 = (pred[2]{0:T(512)(128)(4,1)S(1)}, pred[2]{0:T(512)(128)(4,1)}, u32[]{:S(2)}) copy-start(pred[2]{0:T(512)(128)(4,1)} %get-tuple-element.239) | copy-start | bytes 10
  116.7 15.4 %copy-start.142 = (pred[2]{0:T(512)(128)(4,1)S(1)}, pred[2]{0:T(512)(128)(4,1)}, u32[]{:S(2)}) copy-start(pred[2]{0:T(512)(128)(4,1)} %get-tuple-element.240) | copy-start | bytes 10
  116.7 16.1 %copy-start.151 = (pred[2]{0:T(512)(128)(4,1)S(1)}, pred[2]{0:T(512)(128)(4,1)}, u32[]{:S(2)}) copy-start(pred[2]{0:T(512)(128)(4,1)} %get-tuple-element.241) | copy-start | bytes 10
  117.4 16.0 %copy-start.150 = (pred[2]{0:T(512)(128)(4,1)S(1)}, pred[2]{0:T(512)(128)(4,1)}, u32[]{:S(2)}) copy-start(pred[2]{0:T(512)(128)(4,1)} %get-tuple-element.242) | copy-start | bytes 10
  118.1 16.0 %copy-start.149 = (pred[2]{0:T(512)(128)(4,1)S(1)}, pred[2]{0:T(512)(128)(4,1)}, u32[]{:S(2)}) copy-start(pred[2]{0:T(512)(128)(4,1)} %get-tuple-element.243) | copy-start | bytes 10
  118.1 16.6 %copy-start.148 = (pred[2]{0:T(512)(128)(4,1)S(1)}, pred[2]{0:T(512)(128)(4,1)}, u32[]{:S(2)}) copy-start(pred[2]{0:T(512)(128)(4,1)} %get-tuple-element.244) | copy-start | bytes 10
  118.1 17.2 %copy-start.60 = (bf16[2,64,8,1,8]{1,4,3,2,0:T(8,128)(2,1)S(1)}, bf16[2,64,8,1,8]{1,4,3,2,0:T(8,128)(2,1)}, u32[]{:S(2)}) copy-start(bf16[2,64,8,1,8]{1,4,3,2,0:T(8,128)(2,1)} %copy-done.59) | copy-start | bytes 49156
  118.2 17.2 %copy-start.80 = (bf16[2,64,8,1,1]{1,4,3,2,0:T(2,128)(2,1)S(1)}, bf16[2,64,8,1,1]{1,4,3,2,0:T(2,128)(2,1)}, u32[]{:S(2)}) copy-start(bf16[2,64,8,1,1]{1,4,3,2,0:T(2,128)(2,1)} %copy-done.79) | copy-start | bytes 6148
  118.2 17.2 %copy-start.82 = (bf16[2,64,8,1,1]{1,4,3,2,0:T(2,128)(2,1)S(1)}, bf16[2,64,8,1,1]{1,4,3,2,0:T(2,128)(2,1)}, u32[]{:S(2)}) copy-start(bf16[2,64,8,1,1]{1,4,3,2,0:T(2,128)(2,1)} %copy-done.81) | copy-start | bytes 6148
  177.9 8.5 %copy-start.125 = (pred[2]{0:T(512)(128)(4,1)S(1)}, pred[2]{0:T(512)(128)(4,1)}, u32[]{:S(2)}) copy-start(pred[2]{0:T(512)(128)(4,1)} %get-tuple-element.274) | copy-start | bytes 10
  178.0 9.3 %copy-start.133 = (pred[2]{0:T(512)(128)(4,1)S(1)}, pred[2]{0:T(512)(128)(4,1)}, u32[]{:S(2)}) copy-start(pred[2]{0:T(512)(128)(4,1)} %get-tuple-element.275) | copy-start | bytes 10
  178.0 9.4 %copy-start.73 = (bf16[2,64,8,1,1]{1,4,3,2,0:T(2,128)(2,1)S(1)}, bf16[2,64,8,1,1]{1,4,3,2,0:T(2,128)(2,1)}, u32[]{:S(2)}) copy-start(bf16[2,64,8,1,1]{1,4,3,2,0:T(2,128)(2,1)} %get-tuple-element.198) | copy-start | bytes 6148
  178.0 9.4 %copy-start.75 = (bf16[2,64,8,1,1]{1,4,3,2,0:T(2,128)(2,1)S(1)}, bf16[2,64,8,1,1]{1,4,3,2,0:T(2,128)(2,1)}, u32[]{:S(2)}) copy-start(bf16[2,64,8,1,1]{1,4,3,2,0:T(2,128)(2,1)} %get-tuple-element.194) | copy-start | bytes 6148
  211.6 117.1 %all-reduce.5.cloned.1.call-start = ((), (), s32[]{:S(2)}) async-start(), calls=%async_computation.1 | async-start | bytes 1769472 | tf_op jit(solution)/shard_map/psum | solution.py:112
  218.7 30.3 %copy-start.10 = (bf16[9,64,64]{2,1,0:T(8,128)(2,1)S(1)}, bf16[9,64,64]{2,1,0:T(8,128)(2,1)}, u32[]{:S(2)}) copy-start(bf16[9,64,64]{2,1,0:T(8,128)(2,1)} %get-tuple-element.170) | copy-start | bytes 221188
  (119 other events, 438.9 us)
Sparse Core Ops, SparseCore 0:
  211.7 37.2 all-reduce.2
  252.4 76.2 all-reduce.4
where the time goes:
time: 340 us; the launch traced here: 338 us
  local copies, waits for them, and re-layouts  158 us (46%)
  waiting for transfers between devices  106 us (31%)
  other arithmetic  42.7 us (13%)
  between operations  16.4 us (5%)
  matrix products  7.51 us (2%)
  starting transfers between devices  6.93 us (2%)
    psum x1, waiting for transfers between devices, local(): summed = lax.psum(by_scene, 'space')  76.5 us
    reshape x54, local copies, waits for them, and re-layouts, window(): return volume[:, :, start_x:start_x + 8, start_y:start_y + 8, start_z:sta...  67.4 us
    gather x54, local copies, waits for them, and re-layouts, assemble(): jnp.take(section, places[:, 9 * off_x + 3 * off_y + off_z], axis=0)  39.8 us
    psum x1, waiting for transfers between devices, local(): by_scene = lax.psum(grad_w, 'scene')  29.3 us
    unnamed x383, local copies, waits for them, and re-layouts  26.9 us
    gather x23, other arithmetic  13.7 us
    select_n x54, other arithmetic, assemble(): jnp.take(section, places[:, 9 * off_x + 3 * off_y + off_z], axis=0)  11.8 us
    slice x8, local copies, waits for them, and re-layouts, window(): volume[:, :, start_x:start_x + 8, start_y:start_y + 8, start_z:start_z + 8]  8.44 us
  transfers between devices with their start and end apart: 4, of which 2 were waited for; matrix products, arithmetic and copies ran while one was open for 10% of the time, Pallas kernels for 0%

commit v1 on v0

--- a/solution.py
+++ b/solution.py
@@ -108,7 +108,7 @@
     out_y = (acc_y * mask_wide).astype(jnp.bfloat16)[None]
     out_g = (acc_g * mask_wide).astype(jnp.bfloat16)[None]
     grad_w = jnp.concatenate(partial_w, axis=0) * grad_scale
-    by_scene = lax.psum(grad_w, "scene")
+    by_scene = jnp.sum(lax.all_gather(grad_w, "scene"), axis=0)
     summed = lax.psum(by_scene, "space")
     return (out_y, out_g, summed)
 

time: 340 us -> 333 us (0.979)
  waiting for transfers between devices: 106 us -> 96.2 us
    psum x1 -> x0, waiting for transfers between devices: 29.3 us -> none  [local(): by_scene = lax.psum(grad_w, 'scene')]
    all_gather x0 -> x1, waiting for transfers between devices: none -> 22.6 us  [local(): by_scene = jnp.sum(lax.all_gather(grad_w, 'scene'), axis=0)]
    reduce_sum x0 -> x1, other arithmetic: none -> 3.43 us  [local(): by_scene = jnp.sum(lax.all_gather(grad_w, 'scene'), axis=0)]
    unnamed x383 -> x391, local copies, waits for them, and re-layouts: 26.9 us -> 25.9 us
  transfers between devices with their start and end apart: 4 -> 4, of which waited for: 2 -> 2; matrix products, arithmetic and copies ran while one was open for 10% -> 11% of each run, Pallas kernels for 0% -> 0%
where the time goes in v1:
time: 333 us; the launch traced here: 331 us
  local copies, waits for them, and re-layouts  158 us (47%)
  waiting for transfers between devices  96.2 us (29%)
  other arithmetic  45.9 us (14%)
  between operations  16.3 us (5%)
  matrix products  7.5 us (2%)
  starting transfers between devices  6.93 us (2%)
    psum x1, waiting for transfers between devices, local(): summed = lax.psum(by_scene, 'space')  73.6 us
    reshape x54, local copies, waits for them, and re-layouts, window(): return volume[:, :, start_x:start_x + 8, start_y:start_y + 8, start_z:sta...  67.7 us
    gather x54, local copies, waits for them, and re-layouts, assemble(): jnp.take(section, places[:, 9 * off_x + 3 * off_y + off_z], axis=0)  39.8 us
    unnamed x391, local copies, waits for them, and re-layouts  25.9 us
    all_gather x1, waiting for transfers between devices, local(): by_scene = jnp.sum(lax.all_gather(grad_w, 'scene'), axis=0)  22.6 us
    gather x23, other arithmetic  13.7 us
    select_n x54, other arithmetic, assemble(): jnp.take(section, places[:, 9 * off_x + 3 * off_y + off_z], axis=0)  11.9 us
    slice x8, local copies, waits for them, and re-layouts, window(): volume[:, :, start_x:start_x + 8, start_y:start_y + 8, start_z:start_z + 8]  8.47 us
  transfers between devices with their start and end apart: 4, of which 2 were waited for; matrix products, arithmetic and copies ran while one was open for 11% of the time, Pallas kernels for 0%

profile of v1, /device:TPU:0, one launch (start us, length us, event | category | flops | bytes accessed | tf_op | source)
XLA Modules:
  0.0 331.2 jit_solution(5783279187783766611)
XLA Ops:
  8.3 1.3 fusion.14
  11.0 1.3 collective-permute-start.1
  12.3 5.6 %collective-permute-start = (bf16[2,2,64,512]{2,3,1,0:T(8,128)(2,1)S(1)}, bf16[2,2,64,512]{2,3,1,0:T(8,128)(2,1)S(1)}, u32[]{:S(2)}, u32[]{:S(2)}) collective-permute-start(bf16[2,2,64,512]{2,3,1,0:T(8,128)(2,1)S(1)} %pad_maximum_fusion), channel_id=1, source_target_pairs={{0,4},{4,8},{8,12},{12,16},{16,20},{20,24},{24,28},{1,5},{5,9},{9,... | collective-permute-start | bytes 786440 | tf_op jit(solution)/shard_map/ppermute | solution.py:16
  53.4 1.3 gather_fusion.35
  54.6 1.3 gather_fusion.17
  58.2 1.3 gather_fusion.33
  59.5 1.3 gather_fusion.15
  82.6 1.1 pad_maximum_fusion.3
  85.1 1.5 fusion.23
  88.3 1.7 copy.374
  90.1 1.7 copy.375
  91.8 1.7 copy.376
  93.5 1.7 copy.377
  95.2 1.7 copy.378
  97.0 1.7 copy.379
  98.7 1.7 copy.380
  100.4 1.7 copy.381
  103.1 1.8 copy.385
  104.9 1.6 constant_dynamic-update-slice_fusion.17
  106.4 1.7 copy.386
  108.2 1.7 copy.387
  113.1 1.8 copy.391
  135.7 1.2 fusion.22
  137.0 1.7 copy.406
  138.7 1.6 constant_dynamic-update-slice_fusion.26
  140.2 1.7 copy.407
  142.0 1.7 copy.408
  151.2 1.5 fusion.21
  152.7 1.7 copy.437
  154.4 1.6 constant_dynamic-update-slice_fusion.35
  156.0 1.7 copy.438
  157.7 1.7 copy.439
  159.4 1.7 copy.440
  161.2 1.7 copy.441
  162.9 1.7 copy.442
  164.6 1.7 copy.443
  166.4 1.7 copy.444
  168.1 1.7 copy.445
  170.8 1.1 copy.448
  172.6 1.7 copy.449
  187.6 1.3 fusion.20
  190.7 1.7 copy.464
  203.2 1.8 convolution_bitcast_fusion
  219.4 22.6 %all-gather.2.cloned.1.call-done = f32[4,27,64,64]{3,2,1,0:T(8,128)} async-done(((f32[1,27,64,64]{3,2,1,0:T(8,128)}), f32[4,27,64,64]{3,2,1,0:T(8,128)}) %all-gather.2.cloned.1.call-update) | async-done | bytes 1769488 | tf_op jit(solution)/shard_map/all_gather | solution.py:111
  241.9 3.4 %reduce_sum.9 = f32[27,64,64]{2,1,0:T(8,128)} reduce(f32[4,27,64,64]{3,2,1,0:T(8,128)} %all-gather.2.cloned.1.call-done, f32[]{:T(128)} %constant.81.clone.1), dimensions={0}, to_apply=%region_0.9 | reduce | flops 331776 | bytes 2211844 | tf_op jit(solution)/shard_map/reduce_sum | solution.py:111
  246.3 2.3 fusion.5
  248.6 73.6 %all-reduce.2.cloned.1.call-done = f32[27,64,64]{2,1,0:T(8,128)} async-done(((f32[27,64,64]{2,1,0:T(8,128)}), f32[27,64,64]{2,1,0:T(8,128)}) %all-reduce.2.cloned.1.call-update) | async-done | bytes 442384 | tf_op jit(solution)/shard_map/psum | solution.py:112
  322.1 2.2 copy.609
  (645 shorter events, 138.4 us)
Async XLA Ops:
  7.2 234.8 %all-gather.2.cloned.1.call-start = ((), (), s32[]{:S(2)}) async-start(), calls=%async_computation | async-start | bytes 4423680 | tf_op jit(solution)/shard_map/all_gather | solution.py:111
  10.7 16.2 %copy-start.1 = (bf16[27,64,64]{2,1,0:T(8,128)(2,1)S(1)}, bf16[27,64,64]{2,1,0:T(8,128)(2,1)}, u32[]{:S(2)}) copy-start(bf16[27,64,64]{2,1,0:T(8,128)(2,1)} %param.23) | copy-start | bytes 663556
  11.0 32.7 %collective-permute-start.1 = (bf16[2,2,64,512]{2,3,1,0:T(8,128)(2,1)S(1)}, bf16[2,2,64,512]{2,3,1,0:T(8,128)(2,1)S(1)}, u32[]{:S(2)}, u32[]{:S(2)}) collective-permute-start(bf16[2,2,64,512]{2,3,1,0:T(8,128)(2,1)S(1)} %pad_maximum_fusion), channel_id=1, source_target_pairs={{4,0},{8,4},{12,8},{16,12},{20,16},{24,20},{28,24},{5,1},{9,5},{13... | collective-permute-start | bytes 786440 | tf_op jit(solution)/shard_map/ppermute | solution.py:18
  12.3 31.4 %collective-permute-start = (bf16[2,2,64,512]{2,3,1,0:T(8,128)(2,1)S(1)}, bf16[2,2,64,512]{2,3,1,0:T(8,128)(2,1)S(1)}, u32[]{:S(2)}, u32[]{:S(2)}) collective-permute-start(bf16[2,2,64,512]{2,3,1,0:T(8,128)(2,1)S(1)} %pad_maximum_fusion), channel_id=1, source_target_pairs={{0,4},{4,8},{8,12},{12,16},{16,20},{20,24},{24,28},{1,5},{5,9},{9,... | collective-permute-start | bytes 786440 | tf_op jit(solution)/shard_map/ppermute | solution.py:16
  67.2 9.0 %copy-start.132 = (pred[2]{0:T(512)(128)(4,1)S(1)}, pred[2]{0:T(512)(128)(4,1)}, u32[]{:S(2)}) copy-start(pred[2]{0:T(512)(128)(4,1)} %get-tuple-element.270) | copy-start | bytes 10
  68.6 8.4 %copy-start.126 = (pred[2]{0:T(512)(128)(4,1)S(1)}, pred[2]{0:T(512)(128)(4,1)}, u32[]{:S(2)}) copy-start(pred[2]{0:T(512)(128)(4,1)} %get-tuple-element.271) | copy-start | bytes 10
  68.6 8.5 %copy-start.112 = (bf16[7,64]{1,0:T(8,128)(2,1)S(1)}, bf16[7,64]{1,0:T(8,128)(2,1)}, u32[]{:S(2)}) copy-start(bf16[7,64]{1,0:T(8,128)(2,1)} %get-tuple-element.48) | copy-start | bytes 2692
  68.6 9.2 %copy-start.138 = (pred[2]{0:T(512)(128)(4,1)S(1)}, pred[2]{0:T(512)(128)(4,1)}, u32[]{:S(2)}) copy-start(pred[2]{0:T(512)(128)(4,1)} %get-tuple-element.273) | copy-start | bytes 10
  68.6 9.9 %copy-start.128 = (pred[2]{0:T(512)(128)(4,1)S(1)}, pred[2]{0:T(512)(128)(4,1)}, u32[]{:S(2)}) copy-start(pred[2]{0:T(512)(128)(4,1)} %get-tuple-element.274) | copy-start | bytes 10
  68.6 10.0 %copy-start.111 = (bf16[7,64]{1,0:T(8,128)(2,1)S(1)}, bf16[7,64]{1,0:T(8,128)(2,1)}, u32[]{:S(2)}) copy-start(bf16[7,64]{1,0:T(8,128)(2,1)} %get-tuple-element.49) | copy-start | bytes 2692
  68.6 10.7 %copy-start.136 = (pred[2]{0:T(512)(128)(4,1)S(1)}, pred[2]{0:T(512)(128)(4,1)}, u32[]{:S(2)}) copy-start(pred[2]{0:T(512)(128)(4,1)} %get-tuple-element.275) | copy-start | bytes 10
  68.6 10.7 %copy-start.65 = (bf16[2,64,8]{1,2,0:T(8,128)(2,1)S(1)}, bf16[2,64,8]{1,2,0:T(8,128)(2,1)}, u32[]{:S(2)}) copy-start(bf16[2,64,8]{1,2,0:T(8,128)(2,1)} %gather_fusion.35) | copy-start | bytes 6148
  68.6 10.7 %copy-start.66 = (bf16[2,64,8]{1,2,0:T(8,128)(2,1)S(1)}, bf16[2,64,8]{1,2,0:T(8,128)(2,1)}, u32[]{:S(2)}) copy-start(bf16[2,64,8]{1,2,0:T(8,128)(2,1)} %gather_fusion.17) | copy-start | bytes 6148
  68.6 10.7 %copy-start.161 = (pred[2]{0:T(512)(128)(4,1)S(1)}, pred[2]{0:T(512)(128)(4,1)}, u32[]{:S(2)}) copy-start(pred[2]{0:T(512)(128)(4,1)} %get-tuple-element.245) | copy-start | bytes 10
  69.3 10.7 %copy-start.150 = (pred[2]{0:T(512)(128)(4,1)S(1)}, pred[2]{0:T(512)(128)(4,1)}, u32[]{:S(2)}) copy-start(pred[2]{0:T(512)(128)(4,1)} %get-tuple-element.246) | copy-start | bytes 10
  69.3 10.8 %copy-start.67 = (bf16[2,64,8]{1,2,0:T(8,128)(2,1)S(1)}, bf16[2,64,8]{1,2,0:T(8,128)(2,1)}, u32[]{:S(2)}) copy-start(bf16[2,64,8]{1,2,0:T(8,128)(2,1)} %gather_fusion.33) | copy-start | bytes 6148
  69.4 10.8 %copy-start.68 = (bf16[2,64,8]{1,2,0:T(8,128)(2,1)S(1)}, bf16[2,64,8]{1,2,0:T(8,128)(2,1)}, u32[]{:S(2)}) copy-start(bf16[2,64,8]{1,2,0:T(8,128)(2,1)} %gather_fusion.15) | copy-start | bytes 6148
  69.4 10.8 %copy-start.162 = (pred[2]{0:T(512)(128)(4,1)S(1)}, pred[2]{0:T(512)(128)(4,1)}, u32[]{:S(2)}) copy-start(pred[2]{0:T(512)(128)(4,1)} %get-tuple-element.247) | copy-start | bytes 10
  69.4 11.5 %copy-start.148 = (pred[2]{0:T(512)(128)(4,1)S(1)}, pred[2]{0:T(512)(128)(4,1)}, u32[]{:S(2)}) copy-start(pred[2]{0:T(512)(128)(4,1)} %get-tuple-element.248) | copy-start | bytes 10
  69.4 11.6 %copy-start.147 = (pred[2]{0:T(512)(128)(4,1)S(1)}, pred[2]{0:T(512)(128)(4,1)}, u32[]{:S(2)}) copy-start(pred[2]{0:T(512)(128)(4,1)} %get-tuple-element.249) | copy-start | bytes 10
  103.1 8.4 %copy-start.7 = (bf16[2,64,8,8,8]{1,4,3,2,0:T(8,128)(2,1)S(1)}, bf16[2,64,8,8,8]{1,4,3,2,0:T(8,128)(2,1)}, u32[]{:S(2)}) copy-start(bf16[2,64,8,8,8]{1,4,3,2,0:T(8,128)(2,1)} %get-tuple-element.178) | copy-start | bytes 393220
  112.3 8.7 %copy-start.89 = (bf16[7,64,1,8,1]{1,4,3,2,0:T(2,128)(2,1)S(1)}, bf16[7,64,1,8,1]{1,4,3,2,0:T(2,128)(2,1)}, u32[]{:S(2)}) copy-start(bf16[7,64,1,8,1]{1,4,3,2,0:T(2,128)(2,1)} %get-tuple-element.81) | copy-start | bytes 21508
  113.1 9.2 %copy-start.61 = (bf16[7,64,8,8]{1,0,3,2:T(8,128)(2,1)S(1)}, bf16[7,64,8,8]{1,0,3,2:T(8,128)(2,1)}, u32[]{:S(2)}) copy-start(bf16[7,64,8,8]{1,0,3,2:T(8,128)(2,1)} %get-tuple-element.58) | copy-start | bytes 172036
  113.1 9.2 %copy-start.5 = (bf16[7,64,8,8]{1,3,2,0:T(8,128)(2,1)S(1)}, bf16[7,64,8,8]{1,3,2,0:T(8,128)(2,1)}, u32[]{:S(2)}) copy-start(bf16[7,64,8,8]{1,3,2,0:T(8,128)(2,1)} %get-tuple-element.85) | copy-start | bytes 172036
  115.7 9.4 %copy-start.122 = (bf16[7,64,1,1,1]{1,4,3,2,0:T(2,128)(2,1)S(1)}, bf16[7,64,1,1,1]{1,4,3,2,0:T(2,128)(2,1)}, u32[]{:S(2)}) copy-start(bf16[7,64,1,1,1]{1,4,3,2,0:T(2,128)(2,1)} %get-tuple-element.72) | copy-start | bytes 2692
  115.7 9.4 %copy-start.123 = (bf16[7,64,1,1,1]{1,4,3,2,0:T(2,128)(2,1)S(1)}, bf16[7,64,1,1,1]{1,4,3,2,0:T(2,128)(2,1)}, u32[]{:S(2)}) copy-start(bf16[7,64,1,1,1]{1,4,3,2,0:T(2,128)(2,1)} %get-tuple-element.73) | copy-start | bytes 2692
  115.7 10.1 %copy-start.108 = (bf16[7,64]{1,0:T(8,128)(2,1)S(1)}, bf16[7,64]{1,0:T(8,128)(2,1)}, u32[]{:S(2)}) copy-start(bf16[7,64]{1,0:T(8,128)(2,1)} %get-tuple-element.44) | copy-start | bytes 2692
  115.7 10.8 %copy-start.93 = (bf16[7,64,8]{1,0,2:T(8,128)(2,1)S(1)}, bf16[7,64,8]{1,0,2:T(8,128)(2,1)}, u32[]{:S(2)}) copy-start(bf16[7,64,8]{1,0,2:T(8,128)(2,1)} %get-tuple-element.50) | copy-start | bytes 21508
  115.7 10.8 %copy-start.74 = (bf16[7,64,8]{1,2,0:T(8,128)(2,1)S(1)}, bf16[7,64,8]{1,2,0:T(8,128)(2,1)}, u32[]{:S(2)}) copy-start(bf16[7,64,8]{1,2,0:T(8,128)(2,1)} %get-tuple-element.78) | copy-start | bytes 21508
  115.7 12.9 %copy-start.107 = (bf16[7,64]{1,0:T(8,128)(2,1)S(1)}, bf16[7,64]{1,0:T(8,128)(2,1)}, u32[]{:S(2)}) copy-start(bf16[7,64]{1,0:T(8,128)(2,1)} %get-tuple-element.42) | copy-start | bytes 2692
  115.7 13.6 %copy-start.159 = (pred[2]{0:T(512)(128)(4,1)S(1)}, pred[2]{0:T(512)(128)(4,1)}, u32[]{:S(2)}) copy-start(pred[2]{0:T(512)(128)(4,1)} %get-tuple-element.236) | copy-start | bytes 10
  115.7 14.2 %copy-start.157 = (pred[2]{0:T(512)(128)(4,1)S(1)}, pred[2]{0:T(512)(128)(4,1)}, u32[]{:S(2)}) copy-start(pred[2]{0:T(512)(128)(4,1)} %get-tuple-element.237) | copy-start | bytes 10
  116.5 14.1 %copy-start.158 = (pred[2]{0:T(512)(128)(4,1)S(1)}, pred[2]{0:T(512)(128)(4,1)}, u32[]{:S(2)}) copy-start(pred[2]{0:T(512)(128)(4,1)} %get-tuple-element.238) | copy-start | bytes 10
  116.5 14.8 %copy-start.156 = (pred[2]{0:T(512)(128)(4,1)S(1)}, pred[2]{0:T(512)(128)(4,1)}, u32[]{:S(2)}) copy-start(pred[2]{0:T(512)(128)(4,1)} %get-tuple-element.239) | copy-start | bytes 10
  116.5 15.4 %copy-start.146 = (pred[2]{0:T(512)(128)(4,1)S(1)}, pred[2]{0:T(512)(128)(4,1)}, u32[]{:S(2)}) copy-start(pred[2]{0:T(512)(128)(4,1)} %get-tuple-element.240) | copy-start | bytes 10
  116.5 16.1 %copy-start.155 = (pred[2]{0:T(512)(128)(4,1)S(1)}, pred[2]{0:T(512)(128)(4,1)}, u32[]{:S(2)}) copy-start(pred[2]{0:T(512)(128)(4,1)} %get-tuple-element.241) | copy-start | bytes 10
  117.2 16.1 %copy-start.154 = (pred[2]{0:T(512)(128)(4,1)S(1)}, pred[2]{0:T(512)(128)(4,1)}, u32[]{:S(2)}) copy-start(pred[2]{0:T(512)(128)(4,1)} %get-tuple-element.242) | copy-start | bytes 10
  117.9 16.0 %copy-start.153 = (pred[2]{0:T(512)(128)(4,1)S(1)}, pred[2]{0:T(512)(128)(4,1)}, u32[]{:S(2)}) copy-start(pred[2]{0:T(512)(128)(4,1)} %get-tuple-element.243) | copy-start | bytes 10
  118.0 16.7 %copy-start.152 = (pred[2]{0:T(512)(128)(4,1)S(1)}, pred[2]{0:T(512)(128)(4,1)}, u32[]{:S(2)}) copy-start(pred[2]{0:T(512)(128)(4,1)} %get-tuple-element.244) | copy-start | bytes 10
  118.0 17.3 %copy-start.64 = (bf16[2,64,8,1,8]{1,4,3,2,0:T(8,128)(2,1)S(1)}, bf16[2,64,8,1,8]{1,4,3,2,0:T(8,128)(2,1)}, u32[]{:S(2)}) copy-start(bf16[2,64,8,1,8]{1,4,3,2,0:T(8,128)(2,1)} %copy-done.63) | copy-start | bytes 49156
  118.0 17.3 %copy-start.84 = (bf16[2,64,8,1,1]{1,4,3,2,0:T(2,128)(2,1)S(1)}, bf16[2,64,8,1,1]{1,4,3,2,0:T(2,128)(2,1)}, u32[]{:S(2)}) copy-start(bf16[2,64,8,1,1]{1,4,3,2,0:T(2,128)(2,1)} %copy-done.83) | copy-start | bytes 6148
  118.0 17.3 %copy-start.86 = (bf16[2,64,8,1,1]{1,4,3,2,0:T(2,128)(2,1)S(1)}, bf16[2,64,8,1,1]{1,4,3,2,0:T(2,128)(2,1)}, u32[]{:S(2)}) copy-start(bf16[2,64,8,1,1]{1,4,3,2,0:T(2,128)(2,1)} %copy-done.85) | copy-start | bytes 6148
  177.8 8.5 %copy-start.129 = (pred[2]{0:T(512)(128)(4,1)S(1)}, pred[2]{0:T(512)(128)(4,1)}, u32[]{:S(2)}) copy-start(pred[2]{0:T(512)(128)(4,1)} %get-tuple-element.274) | copy-start | bytes 10
  177.8 9.3 %copy-start.137 = (pred[2]{0:T(512)(128)(4,1)S(1)}, pred[2]{0:T(512)(128)(4,1)}, u32[]{:S(2)}) copy-start(pred[2]{0:T(512)(128)(4,1)} %get-tuple-element.275) | copy-start | bytes 10
  177.8 9.4 %copy-start.77 = (bf16[2,64,8,1,1]{1,4,3,2,0:T(2,128)(2,1)S(1)}, bf16[2,64,8,1,1]{1,4,3,2,0:T(2,128)(2,1)}, u32[]{:S(2)}) copy-start(bf16[2,64,8,1,1]{1,4,3,2,0:T(2,128)(2,1)} %get-tuple-element.198) | copy-start | bytes 6148
  177.8 9.4 %copy-start.79 = (bf16[2,64,8,1,1]{1,4,3,2,0:T(2,128)(2,1)S(1)}, bf16[2,64,8,1,1]{1,4,3,2,0:T(2,128)(2,1)}, u32[]{:S(2)}) copy-start(bf16[2,64,8,1,1]{1,4,3,2,0:T(2,128)(2,1)} %get-tuple-element.194) | copy-start | bytes 6148
  209.4 112.7 %all-reduce.2.cloned.1.call-start = ((), (), s32[]{:S(2)}) async-start(), calls=%async_computation.1 | async-start | bytes 1769472 | tf_op jit(solution)/shard_map/psum | solution.py:112
  219.4 26.0 %copy-start.10 = (bf16[9,64,64]{2,1,0:T(8,128)(2,1)S(1)}, bf16[9,64,64]{2,1,0:T(8,128)(2,1)}, u32[]{:S(2)}) copy-start(bf16[9,64,64]{2,1,0:T(8,128)(2,1)} %get-tuple-element.170) | copy-start | bytes 221188
  (123 other events, 460.2 us)
Sparse Core Ops, SparseCore 0:
  209.6 32.3 all-gather.1
  246.0 76.1 all-reduce.1
